TPU v7x, 32 devices: a whole 2x2x4 slice. The times are simulated.
32 devices in a mesh: rep: 2 (over y), head: 4 (over x, core), row: 4 (over z).
Axes of the slice: x: 2, y: 2, z: 4, core: 2. Of those that a mesh axis runs over, the one named last changes fastest.
Arguments:
- hidden: bfloat16 [256, 2, 8192], P(('rep', 'row'), None, 'head'), parts along dimension 0, may hold values from -6 to 6
- input_norm_scale: float32 [8192], P('head'), may hold values from 0.5 to 1.5
- projection_signal: bfloat16 [8192, 4096], P('row', 'head'), may hold values from -0.0625 to 0.0625
- projection_gate: bfloat16 [8192, 4096], P('row', 'head'), may hold values from -0.0625 to 0.0625
- projection_step: bfloat16 [8192, 64], P('row', 'head'), may hold values from -0.0625 to 0.0625
- projection_input_output: bfloat16 [8192, 256], P('row'), may hold values from -0.0625 to 0.0625
- step_bias: float32 [64], P('head'), may hold values from -4 to 0
- head_decay_rate: float32 [64], P('head'), may hold values from 0.5 to 16
- head_skip_weight: float32 [64], P('head'), may hold values from 0.5 to 1.5
- gated_norm_scale: float32 [4096], P('head'), may hold values from 0.5 to 1.5
- adapter_down_weight: bfloat16 [512, 8192, 16], P('row', 'head'), may hold values from -0.0625 to 0.0625
- adapter_up_weight: bfloat16 [512, 16, 4096], P('row', None, 'head'), may hold values from -1.5 to 1.5
- output_weight: bfloat16 [4096, 8192], P('head'), may hold values from -0.125 to 0.125
- scan_state: bfloat16 [256, 64, 64, 128], P(('rep', 'row'), 'head'), parts along dimension 0, may hold values from -6 to 6
- stream_tenant_index: int32 [256], P(('rep', 'row')), parts along dimension 0, may hold values from 0 to 511, as said below
- live_block_rows: int32 [8], P(('rep', 'row')), parts along dimension 0, may hold values from 1 to 32
Outputs:
- mixed: bfloat16 [256, 2, 8192], P(('rep', 'row'), None, 'head'), parts along dimension 0
- new_state: bfloat16 [256, 64, 64, 128], P(('rep', 'row'), 'head'), parts along dimension 0
There are 2 independent parts, one for each index of `rep`. A program takes and returns all parts, laid end to end along the dimension named above; an argument that names none is the same for every part. Nothing has to cross between parts.
Inputs may be any that keep to these rules, and one draw needn't show every extreme that they name: `stream_tenant_index`: a stream of block b has a tenant of b * 128 up to (b + 1) * 128 - 1.
All inputs are finite; a program needn't handle non-finite values.
Results may differ from a plain program's by a relative error of at most 0.02.
Values may be sent and summed in bfloat16 or wider, within the bound.
A program may use at most 128 MiB of HBM per device.

v0:
```python
import jax
import jax.numpy as jnp
from jax import lax
from jax.sharding import PartitionSpec as P

MODEL_WIDTH = 8192
INNER_WIDTH = 4096


def on_device(
    hidden,
    input_norm_scale,
    projection_signal,
    projection_gate,
    projection_step,
    projection_input_output,
    step_bias,
    head_decay_rate,
    head_skip_weight,
    gated_norm_scale,
    adapter_down_weight,
    adapter_up_weight,
    output_weight,
    scan_state,
    stream_tenant_index,
    live_block_rows,
):
    epsilon = 1e-05
    streams = hidden.shape[0]
    positions = hidden.shape[1]
    inner = projection_signal.shape[1]
    heads_here = projection_step.shape[1]
    state_width = projection_input_output.shape[1] // 2
    feature_width = hidden.shape[2]
    wide = hidden.astype(jnp.float32)
    tenant_local = stream_tenant_index - lax.axis_index("row") * adapter_down_weight.shape[0]
    scaled = (wide * input_norm_scale).astype(jnp.bfloat16)
    down_weight_rows = jnp.take(adapter_down_weight, tenant_local, axis=0)
    square_part = jnp.sum(wide * wide, -1)
    lowrank_part = jnp.einsum(
        "spd,sdr->spr", scaled, down_weight_rows, preferred_element_type=jnp.float32
    )
    squares, lowrank_sum = lax.psum((square_part, lowrank_part), "head")
    inverse = lax.rsqrt(squares / MODEL_WIDTH + epsilon)
    lowrank = (lowrank_sum * inverse[..., None]).astype(jnp.bfloat16)
    normed = (wide * input_norm_scale * inverse[..., None]).astype(jnp.bfloat16)
    features = lax.all_gather(normed, "head", axis=2, tiled=True)
    weight_cat = jnp.concatenate(
        [projection_signal, projection_gate, projection_step, projection_input_output], axis=1
    )
    moved = lax.all_to_all(features, "row", split_axis=2, concat_axis=0, tiled=True)
    moved_flat = moved.reshape(-1, moved.shape[2])
    projected = lax.psum_scatter(
        jnp.dot(moved_flat, weight_cat, preferred_element_type=jnp.float32).astype(jnp.bfloat16),
        "row",
        scatter_dimension=0,
        tiled=True,
    ).astype(jnp.float32)
    projected = projected.reshape(streams, positions, -1)
    xin = projected[..., :inner]
    zin = projected[..., inner : 2 * inner]
    dtin = projected[..., 2 * inner : 2 * inner + heads_here]
    bcin = projected[..., 2 * inner + heads_here :]
    up_weight_rows = jnp.take(adapter_up_weight, tenant_local, axis=0)
    signal = jax.nn.silu(
        xin
        + jnp.einsum("spr,srk->spk", lowrank, up_weight_rows, preferred_element_type=jnp.float32)
    )
    bgate = jax.nn.silu(bcin[..., :state_width])
    cgate = jax.nn.silu(bcin[..., state_width:])
    steps_dt = jax.nn.softplus(dtin + step_bias)
    decay = jnp.exp(-steps_dt * head_decay_rate)
    live = jnp.arange(streams) < live_block_rows[0]
    signal_heads = signal.reshape(streams, positions, heads_here, -1)
    carried = scan_state.astype(jnp.float32)
    outputs = []
    for position in range(positions):
        updated = (
            carried * decay[:, position, :, None, None]
            + (steps_dt[:, position, :, None] * signal_heads[:, position])[..., None]
            * bgate[:, position, None, None, :]
        )
        carried = jnp.where(live[:, None, None, None], updated, carried)
        outputs.append(
            jnp.sum(carried * cgate[:, position, None, None, :], -1)
            + head_skip_weight[None, :, None] * signal_heads[:, position]
        )
    new_state = carried.astype(jnp.bfloat16)
    result = jnp.stack(outputs, 1).reshape(streams, positions, inner)
    gated = result * jax.nn.silu(zin)
    gate_squares = lax.psum(jnp.sum(gated * gated, -1), "head")
    outnorm = (
        gated * lax.rsqrt(gate_squares / INNER_WIDTH + epsilon)[..., None] * gated_norm_scale
    ).astype(jnp.bfloat16)
    out_flat = outnorm.reshape(streams * positions, inner)
    partial_out = jnp.dot(out_flat, output_weight, preferred_element_type=jnp.float32)
    mixer = lax.psum_scatter(
        partial_out.astype(jnp.bfloat16), "head", scatter_dimension=1, tiled=True
    ).astype(jnp.float32)
    mixer = mixer.reshape(streams, positions, feature_width)
    mixed = (wide + jnp.where(live[:, None, None], mixer, 0.0)).astype(jnp.bfloat16)
    return (mixed, new_state)


def solution(mesh):
    in_specs = (
        P(("rep", "row"), None, "head"),
        P("head"),
        P("row", "head"),
        P("row", "head"),
        P("row", "head"),
        P("row", None),
        P("head"),
        P("head"),
        P("head"),
        P("head"),
        P("row", "head", None),
        P("row", None, "head"),
        P("head", None),
        P(("rep", "row"), "head", None, None),
        P(("rep", "row")),
        P(("rep", "row")),
    )
    out_specs = (P(("rep", "row"), None, "head"), P(("rep", "row"), "head", None, None))
    return jax.shard_map(
        on_device, mesh=mesh, in_specs=in_specs, out_specs=out_specs, check_vma=False
    )
```

profile of v0, /device:TPU:0, one launch (start us, length us, event | category | flops | bytes accessed | tf_op | source)
XLA Modules:
  0.0 219.4 jit_solution(15513517323388367327)
XLA Ops:
  7.2 0.7 compare_and_fusion
  7.9 4.1 %gather_fusion = bf16[32,2048,16]{1,2,0:T(8,128)(2,1)S(1)} fusion(bf16[128,2048,16]{1,2,0:T(8,128)(2,1)} %param.26, s32[1024]{0:T(1024)S(1)} %pad_clamp_fusion), kind=kCustom, calls=%fused_computation | custom fusion | bytes 4194432 | tf_op jit(solution)/shard_map/jit(_take)/gather | solution.py:38
  12.2 1.0 fusion.2
  13.3 13.8 %all-reduce = (f32[32,2]{0,1:T(2,128)S(1)}, f32[32,2,16]{2,1,0:T(2,128)}) all-reduce(f32[32,2]{0,1:T(2,128)S(1)} %get-tuple-element.32, f32[32,2,16]{2,1,0:T(2,128)S(1)} %fusion.2), channel_id=1, replica_groups=mesh['rep'=2,'head'=4,'row'=4] {'head'}, use_global_device_ids=true, to_apply=%region_1.2 | all-reduce | flops 1088 | bytes 8704 | tf_op jit(solution)/shard_map/psum | solution.py:43
  27.0 0.8 fusion.10
  27.9 17.2 %all-gather.2.cloned.1.call-done = bf16[32,2,8192]{2,0,1:T(8,128)(2,1)} async-done(((bf16[32,2,2048]{2,0,1:T(8,128)(2,1)}), bf16[32,2,8192]{2,0,1:T(8,128)(2,1)}) %all-gather.2.cloned.1.call-update) | async-done | bytes 1048592 | tf_op jit(solution)/shard_map/all_gather | solution.py:47
  45.0 9.2 %copy.76 = bf16[32,2,8192]{0,1,2:T(2,128)(2,1)} copy(bf16[32,2,8192]{2,0,1:T(8,128)(2,1)} %all-gather.2.cloned.1.call-done) | data formatting | bytes 2097152 | tf_op jit(solution)/shard_map/all_gather | solution.py:47
  54.2 6.4 %reshape.98 = bf16[4,2,65536]{2,1,0:T(2,128)(2,1)} reshape(bf16[8192,2,32]{2,1,0:T(2,128)(2,1)} %bitcast.34) | data formatting | bytes 2097152
  60.6 4.6 %all-to-all-start = ((bf16[4,2,65536]{2,1,0:T(2,128)(2,1)}), bf16[4,2,65536]{2,1,0:T(2,128)(2,1)S(1)}, u32[]{:S(2)}, u32[]{:S(2)}) async-start(bf16[4,2,65536]{2,1,0:T(2,128)(2,1)} %reshape.98), calls=%async_computation | async-start | bytes 2097152 | tf_op jit(solution)/shard_map/all_to_all | solution.py:51
  65.5 15.0 %concatenate.4 = bf16[2048,2320]{1,0:T(8,128)(2,1)} concatenate(bf16[2048,1024]{1,0:T(8,128)(2,1)} %param.18, bf16[2048,1024]{1,0:T(8,128)(2,1)} %param.19, bf16[2048,16]{1,0:T(8,128)(2,1)S(1)} %copy.78, bf16[2048,256]{1,0:T(8,128)(2,1)S(1)} %copy-done.1), dimensions={1} | concatenate | bytes 19005440 | tf_op jit(solution)/shard_map/concatenate | solution.py:48
  80.5 10.8 %all-to-all-done = bf16[4,2,65536]{2,1,0:T(2,128)(2,1)S(1)} async-done(((bf16[4,2,65536]{2,1,0:T(2,128)(2,1)}), bf16[4,2,65536]{2,1,0:T(2,128)(2,1)S(1)}, u32[]{:S(2)}, u32[]{:S(2)}) %all-to-all-start) | async-done | bytes 1048608 | tf_op jit(solution)/shard_map/all_to_all | solution.py:51
  91.3 3.5 %reshape.99 = bf16[8192,2,32]{2,1,0:T(2,128)(2,1)} reshape(bf16[4,2,65536]{2,1,0:T(2,128)(2,1)S(1)} %all-to-all-done) | data formatting | bytes 2097152
  94.7 9.7 %copy.77 = bf16[32,2,4,2048]{3,1,0,2:T(2,128)(2,1)S(1)} copy(bf16[32,2,4,2048]{0,1,3,2:T(2,128)(2,1)} %bitcast.35) | data formatting | bytes 2097152 | tf_op jit(solution)/shard_map/all_to_all | solution.py:51
  104.9 7.7 %convolution_convert_fusion.1 = bf16[256,2320]{1,0:T(8,128)(2,1)} fusion(bf16[256,2048]{1,0:T(8,128)(2,1)S(1)} %reshape.69, bf16[2048,2320]{1,0:T(8,128)(2,1)} %concatenate.4), kind=kOutput, calls=%fused_computation.10 | convolution fusion | flops 2433290240 | bytes 11739136 | tf_op jit(solution)/shard_map/dot_general | solution.py:54
  112.8 2.8 %gather_fusion.1 = bf16[32,16,1024]{2,1,0:T(8,128)(2,1)S(1)} fusion(bf16[128,16,1024]{2,1,0:T(8,128)(2,1)} %param.27, s32[1024]{0:T(1024)S(1)} %pad_clamp_fusion), kind=kCustom, calls=%fused_computation.1 | custom fusion | bytes 2097280 | tf_op jit(solution)/shard_map/jit(_take)/gather | solution.py:64
  116.3 25.0 %reduce-scatter.3.cloned.1.call-done = bf16[64,2320]{1,0:T(8,128)(2,1)} async-done(((bf16[256,2320]{1,0:T(8,128)(2,1)}), bf16[64,2320]{1,0:T(8,128)(2,1)}) %reduce-scatter.3.cloned.1.call-update) | async-done | bytes 296976 | tf_op jit(solution)/shard_map/reduce_scatter | solution.py:53
  141.3 1.3 reshape.77
  144.4 24.9 %multiply_reduce_fusion.1 = (f32[32,16,64]{2,1,0:T(8,128)S(1)}, f32[32,16,64]{2,1,0:T(8,128)S(1)}, bf16[32,16,64,128]{3,2,1,0:T(8,128)(2,1)}) fusion(bf16[32,16,64,128]{3,2,1,0:T(8,128)(2,1)} %param.29, f32[32,128]{1,0:T(8,128)S(1)} %bitcast.39, f32[32,128]{1,0:T(8,128)S(1)} %bitcast.38, f32[32,16,64]{2,1,0:T(8,128)S(1)} %get-tuple-element.30, ...), kind=kLoop, calls=%fused_computation.7 | loop fusion | flops 58654720 | bytes 17371168 | tf_op jit(solution)/shard_map/reduce_sum | solution.py:85
  169.8 0.6 multiply_reduce_fusion.2
  170.4 6.3 %psum.23 = f32[32,2]{0,1:T(2,128)S(1)} all-reduce(f32[32,2]{0,1:T(2,128)S(1)} %copy.86), channel_id=1, replica_groups=mesh['rep'=2,'head'=4,'row'=4] {'head'}, use_global_device_ids=true, to_apply=%region_7.8 | all-reduce | flops 64 | bytes 512 | tf_op jit(solution)/shard_map/psum | solution.py:91
  177.1 9.8 %convolution_convert_fusion = bf16[64,8192]{1,0:T(8,128)(2,1)} fusion(bf16[64,1024]{1,0:T(8,128)(2,1)S(1)} %reshape.73, bf16[1024,8192]{1,0:T(8,128)(2,1)} %param.28), kind=kOutput, calls=%fused_computation.9 | convolution fusion | flops 1074266112 | bytes 17956864 | tf_op jit(solution)/shard_map/dot_general | solution.py:96
  186.9 23.3 %reduce-scatter.5.cloned.1.call-done = bf16[64,2048]{1,0:T(8,128)(2,1)} async-done(((bf16[64,8192]{1,0:T(8,128)(2,1)}), bf16[64,2048]{1,0:T(8,128)(2,1)}) %reduce-scatter.5.cloned.1.call-update) | async-done | bytes 262160 | tf_op jit(solution)/shard_map/reduce_scatter | solution.py:97
  210.3 1.3 reshape.79
  211.9 1.0 copy.89
  (53 shorter events, 4.2 us)
Async XLA Ops:
  7.2 37.9 %all-gather.2.cloned.1.call-start = ((), (), s32[]{:S(2)}) async-start(), calls=%async_computation.3 | async-start | bytes 1310720 | tf_op jit(solution)/shard_map/all_gather | solution.py:47
  7.9 4.1 %copy-start = (bf16[32,2,2048]{2,1,0:T(2,128)(2,1)S(1)}, bf16[32,2,2048]{2,1,0:T(2,128)(2,1)}, u32[]{:S(2)}) copy-start(bf16[32,2,2048]{2,1,0:T(2,128)(2,1)} %param.16) | copy-start | bytes 786436
  7.9 4.1 %copy-start.3 = (f32[2048]{0:T(1024)S(1)}, f32[2048]{0:T(1024)}, u32[]{:S(2)}) copy-start(f32[2048]{0:T(1024)} %param.17) | copy-start | bytes 24580
  12.0 53.1 %copy-start.2 = (bf16[2048,16]{0,1:T(8,128)(2,1)S(1)}, bf16[2048,16]{0,1:T(8,128)(2,1)}, u32[]{:S(2)}) copy-start(bf16[2048,16]{0,1:T(8,128)(2,1)} %param.20) | copy-start | bytes 196612
  12.1 53.4 %copy-start.1 = (bf16[2048,256]{1,0:T(8,128)(2,1)S(1)}, bf16[2048,256]{1,0:T(8,128)(2,1)}, u32[]{:S(2)}) copy-start(bf16[2048,256]{1,0:T(8,128)(2,1)} %param.21) | copy-start | bytes 3145732
  60.6 30.7 %all-to-all-start = ((bf16[4,2,65536]{2,1,0:T(2,128)(2,1)}), bf16[4,2,65536]{2,1,0:T(2,128)(2,1)S(1)}, u32[]{:S(2)}, u32[]{:S(2)}) async-start(bf16[4,2,65536]{2,1,0:T(2,128)(2,1)} %reshape.98), calls=%async_computation | async-start | bytes 2097152 | tf_op jit(solution)/shard_map/all_to_all | solution.py:51
  65.2 76.1 %reduce-scatter.3.cloned.1.call-start = ((), (), s32[]{:S(2)}) async-start(), calls=%async_computation.4 | async-start | bytes 1556480 | tf_op jit(solution)/shard_map/reduce_scatter | solution.py:53
  104.9 37.9 %copy-start.8 = (f32[32,2,16]{2,1,0:T(2,128)S(1)}, f32[32,2,16]{2,1,0:T(2,128)}, u32[]{:S(2)}) copy-start(f32[32,2,16]{2,1,0:T(2,128)} %get-tuple-element.17) | copy-start | bytes 12292
  112.6 31.0 %copy-start.5 = (f32[16]{0:T(128)S(1)}, f32[16]{0:T(128)}, u32[]{:S(2)}) copy-start(f32[16]{0:T(128)} %param.23) | copy-start | bytes 196
  112.6 31.0 %copy-start.6 = (f32[16]{0:T(128)S(1)}, f32[16]{0:T(128)}, u32[]{:S(2)}) copy-start(f32[16]{0:T(128)} %param.22) | copy-start | bytes 196
  112.7 97.6 %reduce-scatter.5.cloned.1.call-start = ((), (), s32[]{:S(2)}) async-start(), calls=%async_computation.5 | async-start | bytes 1310720 | tf_op jit(solution)/shard_map/reduce_scatter | solution.py:97
  143.3 26.0 %copy-start.7 = (f32[16]{0:T(128)S(1)}, f32[16]{0:T(128)}, u32[]{:S(2)}) copy-start(f32[16]{0:T(128)} %param.24) | copy-start | bytes 196
  144.4 32.5 %copy-start.4 = (f32[1024]{0:T(1024)S(1)}, f32[1024]{0:T(1024)}, u32[]{:S(2)}) copy-start(f32[1024]{0:T(1024)} %param.25) | copy-start | bytes 12292
Sparse Core Ops, SparseCore 0:
  28.0 17.0 all-gather.1
  112.8 28.4 reduce-scatter.2
  187.0 23.1 reduce-scatter.4
where the time goes:
time: 221 us; the launch traced here: 219 us
  waiting for transfers between devices  76.4 us (35%)
  local copies, waits for them, and re-layouts  56.3 us (25%)
  other arithmetic  28.3 us (13%)
  blocking collectives  20.1 us (9%)
  matrix products  19 us (9%)
  between operations  14.6 us (7%)
  starting transfers between devices  4.68 us (2%)
    reduce_scatter x1, waiting for transfers between devices, on_device(): lax.psum_scatter(jnp.dot(moved_flat, weight_cat, preferred_element_type=j...  25 us
    reduce_sum x1, other arithmetic, on_device(): jnp.sum(carried * cgate[:, position, None, None, :], -1)  24.9 us
    reduce_scatter x1, waiting for transfers between devices, on_device(): lax.psum_scatter(partial_out.astype(jnp.bfloat16), 'head', scatter_dimens...  23.3 us
    all_gather x1, waiting for transfers between devices, on_device(): features = lax.all_gather(normed, 'head', axis=2, tiled=True)  17.2 us
    concatenate x1, local copies, waits for them, and re-layouts, on_device(): jnp.concatenate([projection_signal, projection_gate, projection_step, pro...  15 us
    psum x1, blocking collectives, on_device(): squares, lowrank_sum = lax.psum((square_part, lowrank_part), 'head')  13.8 us
    unnamed x23, local copies, waits for them, and re-layouts  11.2 us
    all_to_all x1, waiting for transfers between devices, on_device(): lax.all_to_all(features, 'row', split_axis=2, concat_axis=0, tiled=True)  10.8 us
  transfers between devices with their start and end apart: 4, of which 4 were waited for; matrix products, arithmetic and copies ran while one was open for 8% of the time, Pallas kernels for 0%

commit v1 on v0

--- a/solution.py
+++ b/solution.py
@@ -48,7 +48,10 @@
     weight_cat = jnp.concatenate(
         [projection_signal, projection_gate, projection_step, projection_input_output], axis=1
     )
-    moved = lax.all_to_all(features, "row", split_axis=2, concat_axis=0, tiled=True)
+    n_dev = lax.axis_size("row")
+    shards = jnp.stack(jnp.split(features, n_dev, axis=2), axis=0)
+    shards = lax.all_to_all(shards, "row", split_axis=0, concat_axis=0)
+    moved = jnp.concatenate(shards, axis=0)
     moved_flat = moved.reshape(-1, moved.shape[2])
     projected = lax.psum_scatter(
         jnp.dot(moved_flat, weight_cat, preferred_element_type=jnp.float32).astype(jnp.bfloat16),

time: 221 us -> 202 us (0.914)
  local copies, waits for them, and re-layouts: 56.3 us -> 28.6 us
  other arithmetic: 28.3 us -> 33 us
  blocking collectives: 20.1 us -> 24.3 us
    unnamed x23 -> x20, local copies, waits for them, and re-layouts: 11.2 us -> 0.39 us
    all_to_all x1 -> x0, local copies, waits for them, and re-layouts: 9.69 us -> none  [on_device(): lax.all_to_all(features, 'row', split_axis=2, concat_axis=0, tiled=True)]
    all_gather x1 -> x0, local copies, waits for them, and re-layouts: 9.15 us -> none  [on_device(): features = lax.all_gather(normed, 'head', axis=2, tiled=True)]
    psum x1, blocking collectives: 6.33 us -> 10.5 us  [on_device(): gate_squares = lax.psum(jnp.sum(gated * gated, -1), 'head')]
    another operation x0 -> x1, other arithmetic: none -> 2.74 us  [on_device(): shards = jnp.stack(jnp.split(features, n_dev, axis=2), axis=0)]
    another operation x0 -> x2, local copies, waits for them, and re-layouts: none -> 2.62 us  [the longest x1 2.2 us: on_device(): shards = jnp.stack(jnp.split(features, n_dev, axis=2), axis=0)]
  transfers between devices with their start and end apart: 4 -> 4, of which waited for: 4 -> 4; matrix products, arithmetic and copies ran while one was open for 8% -> 9% of each run, Pallas kernels for 0% -> 0%
where the time goes in v1:
time: 202 us; the launch traced here: 201 us
  waiting for transfers between devices  76.5 us (38%)
  other arithmetic  33 us (16%)
  local copies, waits for them, and re-layouts  28.6 us (14%)
  blocking collectives  24.3 us (12%)
  matrix products  19 us (9%)
  between operations  14.6 us (7%)
  starting transfers between devices  4.68 us (2%)
    reduce_scatter x1, waiting for transfers between devices, on_device(): lax.psum_scatter(jnp.dot(moved_flat, weight_cat, preferred_element_type=j...  25.1 us
    reduce_sum x1, other arithmetic, on_device(): jnp.sum(carried * cgate[:, position, None, None, :], -1)  24.9 us
    reduce_scatter x1, waiting for transfers between devices, on_device(): lax.psum_scatter(partial_out.astype(jnp.bfloat16), 'head', scatter_dimens...  23.4 us
    all_gather x1, waiting for transfers between devices, on_device(): features = lax.all_gather(normed, 'head', axis=2, tiled=True)  17.2 us
    concatenate x1, local copies, waits for them, and re-layouts, on_device(): jnp.concatenate([projection_signal, projection_gate, projection_step, pro...  15 us
    psum x1, blocking collectives, on_device(): squares, lowrank_sum = lax.psum((square_part, lowrank_part), 'head')  13.8 us
    all_to_all x1, waiting for transfers between devices, on_device(): shards = lax.all_to_all(shards, 'row', split_axis=0, concat_axis=0)  10.8 us
    psum x1, blocking collectives, on_device(): gate_squares = lax.psum(jnp.sum(gated * gated, -1), 'head')  10.5 us
  transfers between devices with their start and end apart: 4, of which 4 were waited for; matrix products, arithmetic and copies ran while one was open for 9% of the time, Pallas kernels for 0%

profile of v1, /device:TPU:0, one launch (start us, length us, event | category | flops | bytes accessed | tf_op | source)
XLA Modules:
  0.0 200.8 jit_solution(208756091860985009)
XLA Ops:
  7.2 0.7 compare_and_fusion
  7.9 1.3 fusion.11
  9.2 4.1 %gather_fusion = bf16[32,2048,16]{1,2,0:T(8,128)(2,1)S(1)} fusion(bf16[128,2048,16]{1,2,0:T(8,128)(2,1)} %param.26, s32[1024]{0:T(1024)S(1)} %pad_clamp_fusion), kind=kCustom, calls=%fused_computation | custom fusion | bytes 4194432 | tf_op jit(solution)/shard_map/jit(_take)/gather | solution.py:38
  13.4 1.0 fusion.2
  14.4 13.8 %all-reduce = (f32[32,2]{1,0:T(8,128)S(1)}, f32[32,2,16]{2,1,0:T(2,128)}) all-reduce(f32[32,2]{1,0:T(8,128)S(1)} %fusion.11, f32[32,2,16]{2,1,0:T(2,128)S(1)} %fusion.2), channel_id=1, replica_groups=mesh['rep'=2,'head'=4,'row'=4] {'head'}, use_global_device_ids=true, to_apply=%region_1.2 | all-reduce | flops 1088 | bytes 8704 | tf_op jit(solution)/shard_map/psum | solution.py:43
  28.2 1.0 fusion.10
  29.2 17.2 %all-gather.2.cloned.1.call-done = bf16[32,2,8192]{2,1,0:T(2,128)(2,1)} async-done(((bf16[32,2,2048]{2,1,0:T(2,128)(2,1)}), bf16[32,2,8192]{2,1,0:T(2,128)(2,1)}) %all-gather.2.cloned.1.call-update) | async-done | bytes 1048592 | tf_op jit(solution)/shard_map/all_gather | solution.py:47
  46.4 2.2 %slice_bitcast_fusion.3 = (bf16[1,32,2,2048]{3,2,1,0:T(2,128)(2,1)S(1)}, bf16[1,32,2,2048]{3,2,1,0:T(2,128)(2,1)S(1)}, bf16[1,32,2,2048]{3,2,1,0:T(2,128)(2,1)S(1)}, bf16[1,32,2,2048]{3,2,1,0:T(2,128)(2,1)S(1)}) fusion(bf16[32,2,8192]{2,1,0:T(2,128)(2,1)} %all-gather.2.cloned.1.call-done), kind=kLoop, calls=%fused_computation.34 | loop fusion | bytes 2097152 | tf_op jit(solution)/shard_map/stack | solution.py:52
  48.6 2.7 %pad_maximum_fusion = bf16[4,32,2,2048]{3,2,1,0:T(2,128)(2,1)} fusion(bf16[1,32,2,2048]{3,2,1,0:T(2,128)(2,1)S(1)} %get-tuple-element.14, bf16[1,32,2,2048]{3,2,1,0:T(2,128)(2,1)S(1)} %get-tuple-element.15, bf16[1,32,2,2048]{3,2,1,0:T(2,128)(2,1)S(1)} %get-tuple-element.16, bf16[1,32,2,2048]{3,2,1,0:T(2,128)(2,1)S(1)} %get-tuple-element.13), kind=kLoop, calls=%fused_computation.15 | loop fusion | flops 1572864 | bytes 2097152 | tf_op jit(solution)/shard_map/stack | solution.py:52
  51.4 4.6 %all-to-all-start = ((bf16[4,32,2,2048]{3,2,1,0:T(2,128)(2,1)}), bf16[4,32,2,2048]{3,2,1,0:T(2,128)(2,1)S(1)}, u32[]{:S(2)}, u32[]{:S(2)}) async-start(bf16[4,32,2,2048]{3,2,1,0:T(2,128)(2,1)} %pad_maximum_fusion), calls=%async_computation | async-start | bytes 2097152 | tf_op jit(solution)/shard_map/all_to_all | solution.py:53
  56.2 15.0 %concatenate.4 = bf16[2048,2320]{1,0:T(8,128)(2,1)} concatenate(bf16[2048,1024]{1,0:T(8,128)(2,1)} %param.18, bf16[2048,1024]{1,0:T(8,128)(2,1)} %param.19, bf16[2048,16]{1,0:T(8,128)(2,1)S(1)} %copy.31, bf16[2048,256]{1,0:T(8,128)(2,1)S(1)} %copy-done.1), dimensions={1} | concatenate | bytes 19005440 | tf_op jit(solution)/shard_map/concatenate | solution.py:48
  71.2 10.8 %all-to-all-done = bf16[4,32,2,2048]{3,2,1,0:T(2,128)(2,1)S(1)} async-done(((bf16[4,32,2,2048]{3,2,1,0:T(2,128)(2,1)}), bf16[4,32,2,2048]{3,2,1,0:T(2,128)(2,1)S(1)}, u32[]{:S(2)}, u32[]{:S(2)}) %all-to-all-start) | async-done | bytes 1048608 | tf_op jit(solution)/shard_map/all_to_all | solution.py:53
  82.5 7.8 %convolution_convert_fusion.1 = bf16[256,2320]{1,0:T(8,128)(2,1)} fusion(bf16[256,2048]{1,0:T(8,128)(2,1)S(1)} %reshape_reshape.3, bf16[2048,2320]{1,0:T(8,128)(2,1)} %concatenate.4), kind=kOutput, calls=%fused_computation.10 | convolution fusion | flops 2433290240 | bytes 11739136 | tf_op jit(solution)/shard_map/dot_general | solution.py:57
  90.4 2.8 %gather_fusion.1 = bf16[32,16,1024]{2,1,0:T(8,128)(2,1)S(1)} fusion(bf16[128,16,1024]{2,1,0:T(8,128)(2,1)} %param.27, s32[1024]{0:T(1024)S(1)} %pad_clamp_fusion), kind=kCustom, calls=%fused_computation.1 | custom fusion | bytes 2097280 | tf_op jit(solution)/shard_map/jit(_take)/gather | solution.py:67
  93.8 25.1 %reduce-scatter.3.cloned.1.call-done = bf16[64,2320]{1,0:T(8,128)(2,1)} async-done(((bf16[256,2320]{1,0:T(8,128)(2,1)}), bf16[64,2320]{1,0:T(8,128)(2,1)}) %reduce-scatter.3.cloned.1.call-update) | async-done | bytes 296976 | tf_op jit(solution)/shard_map/reduce_scatter | solution.py:56
  118.9 1.3 reshape.72
  120.8 0.5 divide_multiply_fusion.1
  122.0 24.9 %multiply_reduce_fusion.1 = (f32[32,16,64]{2,1,0:T(8,128)S(1)}, f32[32,16,64]{2,1,0:T(8,128)S(1)}, bf16[32,16,64,128]{3,2,1,0:T(8,128)(2,1)}) fusion(bf16[32,16,64,128]{3,2,1,0:T(8,128)(2,1)} %param.29, f32[32,128]{1,0:T(8,128)S(1)} %bitcast.40, f32[32,128]{1,0:T(8,128)S(1)} %bitcast.39, f32[32,16,64]{2,1,0:T(8,128)S(1)} %get-tuple-element.22, ...), kind=kLoop, calls=%fused_computation.7 | loop fusion | flops 58654720 | bytes 17371168 | tf_op jit(solution)/shard_map/reduce_sum | solution.py:88
  147.4 0.6 multiply_reduce_fusion.2
  148.0 10.5 %psum.23 = f32[32,2]{1,0:T(8,128)S(1)} all-reduce(f32[32,2]{1,0:T(8,128)S(1)} %get-tuple-element.6), channel_id=1, replica_groups=mesh['rep'=2,'head'=4,'row'=4] {'head'}, use_global_device_ids=true, to_apply=%region_7.8 | all-reduce | flops 64 | bytes 512 | tf_op jit(solution)/shard_map/psum | solution.py:94
  158.8 9.8 %convolution_convert_fusion = bf16[64,8192]{1,0:T(8,128)(2,1)} fusion(bf16[64,1024]{1,0:T(8,128)(2,1)S(1)} %reshape.68, bf16[1024,8192]{1,0:T(8,128)(2,1)} %param.28), kind=kOutput, calls=%fused_computation.9 | convolution fusion | flops 1074266112 | bytes 17956864 | tf_op jit(solution)/shard_map/dot_general | solution.py:99
  168.6 23.4 %reduce-scatter.5.cloned.1.call-done = bf16[64,2048]{1,0:T(8,128)(2,1)} async-done(((bf16[64,8192]{1,0:T(8,128)(2,1)}), bf16[64,2048]{1,0:T(8,128)(2,1)}) %reduce-scatter.5.cloned.1.call-update) | async-done | bytes 262160 | tf_op jit(solution)/shard_map/reduce_scatter | solution.py:100
  191.9 1.3 reshape.74
  193.2 1.1 fusion.12
  (47 shorter events, 2.8 us)
Async XLA Ops:
  7.2 39.2 %all-gather.2.cloned.1.call-start = ((), (), s32[]{:S(2)}) async-start(), calls=%async_computation.3 | async-start | bytes 1310720 | tf_op jit(solution)/shard_map/all_gather | solution.py:47
  9.2 4.1 %copy-start = (bf16[32,2,2048]{2,1,0:T(2,128)(2,1)S(1)}, bf16[32,2,2048]{2,1,0:T(2,128)(2,1)}, u32[]{:S(2)}) copy-start(bf16[32,2,2048]{2,1,0:T(2,128)(2,1)} %param.16) | copy-start | bytes 786436
  9.2 4.2 %copy-start.3 = (f32[2048]{0:T(1024)S(1)}, f32[2048]{0:T(1024)}, u32[]{:S(2)}) copy-start(f32[2048]{0:T(1024)} %param.17) | copy-start | bytes 24580
  13.3 42.7 %copy-start.2 = (bf16[2048,16]{0,1:T(8,128)(2,1)S(1)}, bf16[2048,16]{0,1:T(8,128)(2,1)}, u32[]{:S(2)}) copy-start(bf16[2048,16]{0,1:T(8,128)(2,1)} %param.20) | copy-start | bytes 196612
  13.3 42.9 %copy-start.1 = (bf16[2048,256]{1,0:T(8,128)(2,1)S(1)}, bf16[2048,256]{1,0:T(8,128)(2,1)}, u32[]{:S(2)}) copy-start(bf16[2048,256]{1,0:T(8,128)(2,1)} %param.21) | copy-start | bytes 3145732
  51.4 30.7 %all-to-all-start = ((bf16[4,32,2,2048]{3,2,1,0:T(2,128)(2,1)}), bf16[4,32,2,2048]{3,2,1,0:T(2,128)(2,1)S(1)}, u32[]{:S(2)}, u32[]{:S(2)}) async-start(bf16[4,32,2,2048]{3,2,1,0:T(2,128)(2,1)} %pad_maximum_fusion), calls=%async_computation | async-start | bytes 2097152 | tf_op jit(solution)/shard_map/all_to_all | solution.py:53
  56.0 63.0 %reduce-scatter.3.cloned.1.call-start = ((), (), s32[]{:S(2)}) async-start(), calls=%async_computation.4 | async-start | bytes 1556480 | tf_op jit(solution)/shard_map/reduce_scatter | solution.py:56
  82.5 38.0 %copy-start.5 = (f32[16]{0:T(128)S(1)}, f32[16]{0:T(128)}, u32[]{:S(2)}) copy-start(f32[16]{0:T(128)} %param.23) | copy-start | bytes 196
  82.5 38.0 %copy-start.6 = (f32[16]{0:T(128)S(1)}, f32[16]{0:T(128)}, u32[]{:S(2)}) copy-start(f32[16]{0:T(128)} %param.22) | copy-start | bytes 196
  82.5 38.2 %copy-start.8 = (f32[32,2,16]{2,1,0:T(2,128)S(1)}, f32[32,2,16]{2,1,0:T(2,128)}, u32[]{:S(2)}) copy-start(f32[32,2,16]{2,1,0:T(2,128)} %get-tuple-element.5) | copy-start | bytes 12292
  90.3 101.6 %reduce-scatter.5.cloned.1.call-start = ((), (), s32[]{:S(2)}) async-start(), calls=%async_computation.5 | async-start | bytes 1310720 | tf_op jit(solution)/shard_map/reduce_scatter | solution.py:100
  121.3 25.6 %copy-start.7 = (f32[16]{0:T(128)S(1)}, f32[16]{0:T(128)}, u32[]{:S(2)}) copy-start(f32[16]{0:T(128)} %param.24) | copy-start | bytes 196
  122.0 36.5 %copy-start.4 = (f32[1024]{0:T(1024)S(1)}, f32[1024]{0:T(1024)}, u32[]{:S(2)}) copy-start(f32[1024]{0:T(1024)} %param.25) | copy-start | bytes 12292
Sparse Core Ops, SparseCore 0:
  29.4 17.0 all-gather.1
  90.4 28.4 reduce-scatter.2
  168.7 23.2 reduce-scatter.4
